TPU v7x, 32 devices: a whole 2x2x4 slice. The times are simulated.
32 devices in a mesh: seq: 8 (over y, x, core), pipe: 4 (over z).
Axes of the slice: x: 2, y: 2, z: 4, core: 2. Of those that a mesh axis runs over, the one named last changes fastest.
Arguments:
- query_in: bfloat16 [4, 1024, 4096], P('pipe', 'seq'), may hold values from -6 to 6
- key_in: bfloat16 [4, 1024, 4096], P('pipe', 'seq'), may hold values from -6 to 6
- value_in: bfloat16 [4, 1024, 4096], P('pipe', 'seq'), may hold values from -6 to 6
- grad_out: bfloat16 [4, 1024, 4096], P('pipe', 'seq'), may hold values from -6 to 6
- long_filter: float32 [4, 1024, 256], P('pipe', 'seq'), may hold values from -2 to 2, as said below
- short_taps: float32 [4, 3, 3, 4096], P('pipe'), may hold values from -3 to 3
Outputs:
- layer_out: bfloat16 [4, 1024, 4096], P('pipe', 'seq')
- passed_grads: bfloat16 [4, 3, 1024, 4096], P('pipe', None, 'seq')
- filter_grad: float32 [4, 1024, 256], P('pipe', 'seq')
- tap_grads: float32 [4, 3, 3, 4096], P('pipe')
Inputs may be any that keep to these rules, and one draw needn't show every extreme that they name: `long_filter`: one filter for each channel group of each section.
All inputs are finite; a program needn't handle non-finite values.
Results may differ from a plain program's by a relative error of at most 0.005.
Values may be sent and summed in bfloat16 or wider, within the bound.
No kernel may reach another device: no remote copies, remote signals or barrier semaphores. Data moves between devices by JAX's collectives and lax.ppermute only.
A program may use at most 256 MiB of HBM per device.

v0:
```python
import math
import jax
import jax.numpy as jnp
from jax import lax
from jax.sharding import PartitionSpec as P

exact_mode = lax.Precision.HIGHEST


def passed_along(x, axis, by):
    count = lax.axis_size(axis)
    pairs = [(i, i + by) for i in range(count) if 0 <= i + by < count]
    return lax.ppermute(x, axis, pairs)


def counting(length):
    return jnp.arange(length, dtype=jnp.int32)


def matmul(left, right):
    return jnp.dot(left, right, precision=exact_mode, preferred_element_type=jnp.float32)


def phases(row_index, col_index, modulus, direction):
    index_product = row_index[:, None] * col_index[None, :] % modulus
    phase_angle = index_product.astype(jnp.float32) * (-2.0 * math.pi * direction / modulus)
    return (jnp.cos(phase_angle), jnp.sin(phase_angle))


def complex_table(row_index, col_index, modulus, direction, factor):
    cosine_part, sine_part = phases(row_index, col_index, modulus, direction)
    upper = jnp.concatenate([cosine_part, -sine_part], axis=1)
    lower = jnp.concatenate([sine_part, cosine_part], axis=1)
    return jnp.concatenate([upper, lower], axis=0) * factor


def lead_segment(packed, row_index, col_index, modulus, direction, factor):
    in_shape = packed.shape
    flattened = packed.reshape(2 * in_shape[1], -1)
    table = complex_table(row_index, col_index, modulus, direction, factor)
    joined = matmul(table, flattened)
    return joined.reshape((2, row_index.shape[0]) + in_shape[2:])


def middle_segment(packed, row_index, col_index, modulus, direction):
    table = complex_table(row_index, col_index, modulus, direction, 1.0)
    table = table.reshape(2, row_index.shape[0], 2, col_index.shape[0])
    return jnp.einsum(
        "xrzb,zkbw->xkrw", table, packed, precision=exact_mode, preferred_element_type=jnp.float32
    )


def twiddle(packed, row_index, col_index, modulus, direction):
    cosine_part, sine_part = phases(row_index, col_index, modulus, direction)
    cosine_part = cosine_part[:, :, None]
    sine_part = sine_part[:, :, None]
    return jnp.stack(
        [
            packed[0] * cosine_part - packed[1] * sine_part,
            packed[0] * sine_part + packed[1] * cosine_part,
        ]
    )


def pack_pairs(values, pack_block):
    lead_dims = values.shape[:-1]
    split_view = values.reshape(lead_dims + (values.shape[-1] // (2 * pack_block), 2, pack_block))
    return jnp.stack(
        [
            split_view[..., 0, :].reshape(lead_dims + (-1,)),
            split_view[..., 1, :].reshape(lead_dims + (-1,)),
        ]
    )


def unpack_pairs(packed, pack_block):
    lead_dims = packed.shape[1:-1]
    pair_view = packed.reshape((2,) + lead_dims + (packed.shape[-1] // pack_block, pack_block))
    joined = jnp.stack([pair_view[0], pair_view[1]], axis=-2)
    return joined.reshape(lead_dims + (-1,))


def group_table(first_packed, col_count, half_group, groups):
    packed_index = first_packed + counting(col_count)
    return (packed_index[None, :] // half_group == counting(groups)[:, None]).astype(jnp.float32)


def spec_product(first_spec, second_spec):
    return jnp.stack(
        [
            first_spec[0] * second_spec[0] - first_spec[1] * second_spec[1],
            first_spec[0] * second_spec[1] + first_spec[1] * second_spec[0],
        ]
    )


def conj_product(first_spec, second_spec):
    return jnp.stack(
        [
            first_spec[0] * second_spec[0] + first_spec[1] * second_spec[1],
            first_spec[1] * second_spec[0] - first_spec[0] * second_spec[1],
        ]
    )


def spread_groups(spectrum, group_map):
    return jnp.einsum(
        "rktg,gq->rktq",
        spectrum,
        group_map,
        precision=exact_mode,
        preferred_element_type=jnp.float32,
    )


def sum_groups(spectrum, group_map):
    return jnp.einsum(
        "rktq,gq->rktg",
        spectrum,
        group_map,
        precision=exact_mode,
        preferred_element_type=jnp.float32,
    )


def local(query_in, key_in, value_in, grad_out, long_filter, short_taps):
    seq_size = lax.axis_size("seq")
    seq_rank = lax.axis_index("seq")
    rows_dev = query_in.shape[1]
    width = query_in.shape[2]
    groups = long_filter.shape[2]
    half_group = width // groups // 2
    pack_block = half_group // 2
    total_rows = rows_dev * seq_size
    fft_length = 2 * total_rows
    tap_table = short_taps[0]
    stacked_in = jnp.stack([query_in[0], key_in[0], value_in[0]])
    before = passed_along(stacked_in[:, rows_dev - 2 :, :], "seq", 1)
    extended = jnp.concatenate([before, stacked_in], axis=1).astype(jnp.float32)
    featured = tap_table[:, 0, None, :] * extended[:, 2 : 2 + rows_dev, :]
    featured = featured + tap_table[:, 1, None, :] * extended[:, 1 : 1 + rows_dev, :]
    featured = featured + tap_table[:, 2, None, :] * extended[:, 0:rows_dev, :]
    query_feat = featured[0]
    keyed = featured[1]
    valued = featured[2]
    grad_float = grad_out[0].astype(jnp.float32)
    product = (keyed * valued).astype(jnp.bfloat16)
    scaled = (grad_float * query_feat).astype(jnp.bfloat16)
    block_rows = rows_dev // seq_size
    group_map = group_table(0, width // 2, half_group, groups)
    freq_index = (
        (2 * seq_rank + counting(2))[:, None] + 2 * seq_size * counting(rows_dev)[None, :]
    ).reshape(-1)
    whole_filter = lax.all_gather(long_filter[0], "seq", axis=0, tiled=True)
    filter_cos, filter_sin = phases(freq_index, counting(total_rows), fft_length, 1)
    own_spec = jnp.stack(
        [matmul(filter_cos, whole_filter), matmul(filter_sin, whole_filter)]
    ).reshape(2, 2, rows_dev, groups)
    kernel = spread_groups(own_spec, group_map)

    def forward(signal):
        arrived = lax.all_to_all(signal[None], "seq", split_axis=1, concat_axis=0, tiled=True)
        packed = pack_pairs(arrived.astype(jnp.float32), pack_block)
        first_segment = lead_segment(
            packed, counting(2 * seq_size), counting(seq_size), 2 * seq_size, 1, 1.0
        )
        turned = twiddle(
            first_segment,
            counting(2 * seq_size),
            seq_rank * block_rows + counting(block_rows),
            fft_length,
            1,
        )
        gathered = lax.all_to_all(turned, "seq", split_axis=1, concat_axis=2, tiled=True)
        return middle_segment(gathered, counting(rows_dev), counting(rows_dev), rows_dev, 1)

    def inverse(spectrum):
        back_segment = middle_segment(
            spectrum, counting(rows_dev), counting(rows_dev), rows_dev, -1
        )
        turned = twiddle(
            back_segment, 2 * seq_rank + counting(2), counting(rows_dev), fft_length, -1
        )
        arrived = lax.all_to_all(turned, "seq", split_axis=2, concat_axis=1, tiled=True)
        row_data = lead_segment(
            arrived, counting(seq_size), counting(2 * seq_size), 2 * seq_size, -1, 1.0 / fft_length
        )
        spread_back = unpack_pairs(row_data, pack_block)
        return lax.all_to_all(spread_back, "seq", split_axis=0, concat_axis=1, tiled=True)[0]

    prod_spec = forward(product)
    conv_out = inverse(spec_product(prod_spec, kernel))
    scaled_spec = forward(scaled)
    back_out = inverse(conj_product(scaled_spec, kernel))
    cross_spec = sum_groups(conj_product(scaled_spec, prod_spec), group_map)
    cross_real = cross_spec[0].reshape(2 * rows_dev, groups)
    cross_imag = cross_spec[1].reshape(2 * rows_dev, groups)
    layer_out = (query_feat * conv_out).astype(jnp.bfloat16)
    grad_stack = jnp.stack([grad_float * conv_out, back_out * valued, back_out * keyed])
    after_rows = passed_along(grad_stack[:, :2, :].astype(jnp.bfloat16), "seq", -1).astype(
        jnp.float32
    )
    padded = jnp.concatenate([grad_stack, after_rows], axis=1)
    input_grads = tap_table[:, 0, None, :] * padded[:, 0:rows_dev, :]
    input_grads = input_grads + tap_table[:, 1, None, :] * padded[:, 1 : 1 + rows_dev, :]
    input_grads = input_grads + tap_table[:, 2, None, :] * padded[:, 2 : 2 + rows_dev, :]
    input_grads = input_grads.astype(jnp.bfloat16)
    tap_terms = jnp.stack(
        [
            jnp.sum(grad_stack * extended[:, 2 - tap_lag : 2 - tap_lag + rows_dev, :], axis=1)
            for tap_lag in range(3)
        ],
        axis=1,
    )
    tap_grads = lax.psum(tap_terms, "seq") / math.sqrt(total_rows)
    positions = counting(rows_dev * lax.axis_size("seq"))
    cosine_part, sine_part = phases(positions, freq_index, fft_length, -1)
    filter_grad = lax.psum_scatter(
        (matmul(cosine_part, cross_real) - matmul(sine_part, cross_imag)) / fft_length,
        "seq",
        scatter_dimension=0,
        tiled=True,
    ) / math.sqrt(total_rows * 2 * half_group)
    passed_grads = passed_along(input_grads, "pipe", -1)
    return (layer_out[None], passed_grads[None], filter_grad[None], tap_grads[None])


def solution(mesh):
    in_specs = (
        P("pipe", "seq", None),
        P("pipe", "seq", None),
        P("pipe", "seq", None),
        P("pipe", "seq", None),
        P("pipe", "seq", None),
        P("pipe", None, None, None),
    )
    out_specs = (
        P("pipe", "seq", None),
        P("pipe", None, "seq", None),
        P("pipe", "seq", None),
        P("pipe", None, None, None),
    )
    return jax.shard_map(local, mesh=mesh, in_specs=in_specs, out_specs=out_specs, check_vma=False)
```

profile of v0, /device:TPU:0, one launch (start us, length us, event | category | flops | bytes accessed | tf_op | source)
XLA Modules:
  0.0 850.4 jit_solution(6586171705041286776)
XLA Ops:
  20.4 7.1 reduce
  29.1 7.6 all-to-all-start.4
  36.9 15.1 %all-to-all-done.4 = bf16[8,2,32768]{2,1,0:T(2,128)(2,1)S(1)} async-done(((bf16[8,2,32768]{2,1,0:T(2,128)(2,1)}), bf16[8,2,32768]{2,1,0:T(2,128)(2,1)S(1)}, u32[]{:S(2)}, u32[]{:S(2)}) %all-to-all-start.4) | async-done | bytes 1048608 | tf_op jit(solution)/shard_map/all_to_all | solution.py:162
  57.9 8.5 reshape.367
  66.4 11.0 %fusion.148 = (f32[8,16,512,1,4]{1,0,4,3,2:T(8,128)}, f32[8,16,512,1,4]{1,0,4,3,2:T(8,128)}) fusion(f32[8,16,512,2,4]{1,0,4,3,2:T(8,128)} %reshape.367), kind=kLoop, calls=%fused_computation.231 | loop fusion | bytes 4194304 | tf_op jit(solution)/shard_map/slice | solution.py:70
  105.5 39.8 %all-gather.3.cloned.1.call-done = f32[1,1024,256]{2,1,0:T(8,128)} async-done(((f32[1,128,256]{2,1,0:T(8,128)}), f32[1,1024,256]{2,1,0:T(8,128)}) %all-gather.3.cloned.1.call-update) | async-done | bytes 1048592 | tf_op jit(solution)/shard_map/all_gather | solution.py:154
  164.6 7.1 fusion.18
  179.9 7.3 copy.194
  193.3 49.7 %all-to-all-done.6 = f32[2,2,128,2048]{3,0,1,2:T(2,128)} async-done(((f32[2,2,128,2048]{3,0,1,2:T(2,128)}), f32[2,2,128,2048]{3,0,1,2:T(2,128)}, u32[]{:S(2)}, u32[]{:S(2)}) %all-to-all-start.6) | async-done | bytes 4194336 | tf_op jit(solution)/shard_map/all_to_all | solution.py:184
  252.9 8.8 %copy.197 = f32[8,32768]{0,1:T(8,128)} copy(f32[8,32768]{1,0:T(8,128)S(1)} %get-tuple-element.37) | data formatting | bytes 2097152 | tf_op jit(solution)/shard_map/slice | solution.py:79
  261.7 8.8 %copy.198 = f32[8,32768]{0,1:T(8,128)} copy(f32[8,32768]{1,0:T(8,128)S(1)} %get-tuple-element.38) | data formatting | bytes 2097152 | tf_op jit(solution)/shard_map/slice | solution.py:79
  270.6 23.0 %pad_maximum_fusion.1 = f32[8,16,512,2,4]{0,4,2,1,3:T(4,128)} fusion(f32[8,16,512,1,4]{0,4,2,1,3:T(4,128)} %bitcast.249, f32[8,16,512,1,4]{0,4,2,1,3:T(4,128)} %bitcast.247), kind=kLoop, calls=%fused_computation.1 | loop fusion | flops 524288 | bytes 4194304 | tf_op jit(solution)/shard_map/stack | solution.py:79
  293.6 30.4 %copy.199 = f32[8,16,512,2,4]{1,0,4,3,2:T(8,128)} copy(f32[8,16,512,2,4]{0,4,2,1,3:T(4,128)} %pad_maximum_fusion.1) | data formatting | bytes 4194304 | tf_op jit(solution)/shard_map/stack | solution.py:79
  324.0 9.6 %copy.200 = f32[8,16,4096]{2,1,0:T(8,128)S(1)} copy(f32[8,16,4096]{1,0,2:T(8,128)} %bitcast.245) | data formatting | bytes 4194304 | tf_op jit(solution)/shard_map/reshape | solution.py:80
  333.6 29.4 %all_to_all.102 = f32[8,16,4096]{2,1,0:T(8,128)S(1)} all-to-all(f32[8,16,4096]{2,1,0:T(8,128)S(1)} %copy.200), channel_id=1, replica_groups=mesh['seq'=8,'pipe'=4] {'seq'}, dimensions={0} | all-to-all | bytes 4194304 | tf_op jit(solution)/shard_map/all_to_all | solution.py:189
  370.7 8.4 reduce.1
  380.7 18.8 %all_to_all.103 = bf16[8,2,32768]{2,1,0:T(2,128)(2,1)S(1)} all-to-all(bf16[8,2,32768]{2,1,0:T(2,128)(2,1)} %reshape.382), channel_id=1, replica_groups=mesh['seq'=8,'pipe'=4] {'seq'}, dimensions={0} | all-to-all | bytes 2097152 | tf_op jit(solution)/shard_map/all_to_all | solution.py:162
  410.5 10.6 %reshape.366 = f32[8,16,512,2,4]{1,0,4,3,2:T(8,128)} reshape(f32[1,128,4096]{1,2,0:T(8,128)} %copy.159) | data formatting | bytes 4194304 | tf_op jit(solution)/shard_map/convert_element_type | solution.py:163
  421.0 11.0 %fusion.149 = (f32[8,16,512,1,4]{1,0,4,3,2:T(8,128)}, f32[8,16,512,1,4]{1,0,4,3,2:T(8,128)}) fusion(f32[8,16,512,2,4]{1,0,4,3,2:T(8,128)} %reshape.366), kind=kLoop, calls=%fused_computation.232 | loop fusion | bytes 4194304 | tf_op jit(solution)/shard_map/slice | solution.py:70
  453.6 51.9 %all_to_all.104 = f32[2,16,16,2048]{3,2,0,1:T(8,128)S(1)} all-to-all(f32[2,16,16,2048]{3,2,0,1:T(8,128)S(1)} %pad_maximum_fusion.4), channel_id=1, replica_groups=mesh['seq'=8,'pipe'=4] {'seq'}, dimensions={1} | all-to-all | bytes 8388608 | tf_op jit(solution)/shard_map/all_to_all | solution.py:174
  506.5 8.3 fusion.15
  528.0 7.3 copy.173
  535.3 52.8 %all_to_all.105 = f32[2,2,128,2048]{3,0,1,2:T(2,128)S(1)} all-to-all(f32[2,2,128,2048]{3,0,1,2:T(2,128)} %copy.173), channel_id=1, replica_groups=mesh['seq'=8,'pipe'=4] {'seq'}, dimensions={2} | all-to-all | bytes 8388608 | tf_op jit(solution)/shard_map/all_to_all | solution.py:184
  596.7 9.1 %copy.176 = f32[8,32768]{0,1:T(8,128)} copy(f32[8,32768]{1,0:T(8,128)} %get-tuple-element.39) | data formatting | bytes 2097152 | tf_op jit(solution)/shard_map/slice | solution.py:79
  605.8 8.8 %copy.177 = f32[8,32768]{0,1:T(8,128)} copy(f32[8,32768]{1,0:T(8,128)S(1)} %get-tuple-element.40) | data formatting | bytes 2097152 | tf_op jit(solution)/shard_map/slice | solution.py:79
  614.7 23.0 %pad_maximum_fusion = f32[8,16,512,2,4]{0,4,2,1,3:T(4,128)} fusion(f32[8,16,512,1,4]{0,4,2,1,3:T(4,128)} %bitcast.250, f32[8,16,512,1,4]{0,4,2,1,3:T(4,128)} %bitcast.248), kind=kLoop, calls=%fused_computation | loop fusion | flops 524288 | bytes 4194304 | tf_op jit(solution)/shard_map/stack | solution.py:79
  637.7 30.4 %copy.178 = f32[8,16,512,2,4]{1,0,4,3,2:T(8,128)} copy(f32[8,16,512,2,4]{0,4,2,1,3:T(4,128)} %pad_maximum_fusion) | data formatting | bytes 4194304 | tf_op jit(solution)/shard_map/stack | solution.py:79
  668.1 10.6 %copy.179 = f32[8,16,4096]{2,1,0:T(8,128)} copy(f32[8,16,4096]{1,0,2:T(8,128)} %bitcast.246) | data formatting | bytes 4194304 | tf_op jit(solution)/shard_map/reshape | solution.py:80
  690.1 19.8 %all-to-all-done.3 = f32[8,16,4096]{2,1,0:T(8,128)} async-done(((f32[8,16,4096]{2,1,0:T(8,128)}), f32[8,16,4096]{2,1,0:T(8,128)}, u32[]{:S(2)}, u32[]{:S(2)}) %all-to-all-start.3) | async-done | bytes 2097184 | tf_op jit(solution)/shard_map/all_to_all | solution.py:189
  720.9 9.4 %multiply_reduce_fusion.2 = (f32[3,4096]{1,0:T(4,128)S(1)}, f32[3,4096]{1,0:T(4,128)S(1)}, f32[3,4096]{1,0:T(4,128)S(1)}, bf16[3,128,4096]{2,1,0:T(8,128)(2,1)}) fusion(f32[3,130,4096]{2,1,0:T(8,128)S(1)} %bitcast.244, f32[1,128,4096]{2,1,0:T(8,128)} %get-tuple-element.14, f32[1,128,4096]{2,1,0:T(8,128)S(1)} %get-tuple-element.13, ...), kind=kLoop, calls=%fused_computation.11 | loop fusion | flops 21983232 | bytes 41189376 | tf_op jit(solution)/shard_map/reduce_sum | solution.py:210
  745.0 38.3 %reduce-scatter.2.cloned.1.call-done = f32[128,256]{1,0:T(8,128)} async-done(((f32[1024,256]{1,0:T(8,128)}), f32[128,256]{1,0:T(8,128)}) %reduce-scatter.2.cloned.1.call-update) | async-done | bytes 131088 | tf_op jit(solution)/shard_map/reduce_scatter | solution.py:218
  784.8 55.2 %all-reduce.2.cloned.1.call-done = f32[3,3,4096]{2,1,0:T(4,128)} async-done(((f32[3,3,4096]{2,1,0:T(4,128)}), f32[3,3,4096]{2,1,0:T(4,128)}) %all-reduce.2.cloned.1.call-update) | async-done | bytes 147472 | tf_op jit(solution)/shard_map/psum | solution.py:215
  (181 shorter events, 198.1 us)
Async XLA Ops:
  7.2 5.3 copy-start.23
  10.0 3.3 collective-permute-start
  17.0 2.8 copy-start.5
  29.1 22.9 %all-to-all-start.4 = ((bf16[8,2,32768]{2,1,0:T(2,128)(2,1)}), bf16[8,2,32768]{2,1,0:T(2,128)(2,1)S(1)}, u32[]{:S(2)}, u32[]{:S(2)}) async-start(bf16[8,2,32768]{2,1,0:T(2,128)(2,1)} %reshape.384), calls=%async_computation.4 | async-start | bytes 2097152 | tf_op jit(solution)/shard_map/all_to_all | solution.py:162
  98.5 63.6 %all-to-all-start.5 = ((f32[2,16,16,2048]{3,2,0,1:T(8,128)}), f32[2,16,16,2048]{3,2,0,1:T(8,128)}, u32[]{:S(2)}, u32[]{:S(2)}) async-start(f32[2,16,16,2048]{3,2,0,1:T(8,128)} %pad_maximum_fusion.6), calls=%async_computation.5 | async-start | bytes 8388608 | tf_op jit(solution)/shard_map/all_to_all | solution.py:174
  103.1 42.3 %all-gather.3.cloned.1.call-start = ((), (), s32[]{:S(2)}) async-start(), calls=%async_computation.11 | async-start | bytes 1179648 | tf_op jit(solution)/shard_map/all_gather | solution.py:154
  104.6 60.0 %copy-start.10 = (f32[2,128,2,128]{3,2,1,0:T(2,128)}, f32[2,128,2,128]{3,2,1,0:T(2,128)S(1)}, u32[]{:S(2)}) copy-start(f32[2,128,2,128]{3,2,1,0:T(2,128)S(1)} %reshape.359) | copy-start | bytes 786436
  105.3 68.5 %copy-start.12 = (f32[2,128,2,128]{3,2,1,0:T(2,128)}, f32[2,128,2,128]{3,2,1,0:T(2,128)S(1)}, u32[]{:S(2)}) copy-start(f32[2,128,2,128]{3,2,1,0:T(2,128)S(1)} %reshape.360) | copy-start | bytes 786436
  105.3 53.1 %copy-start.24 = (s32[2048]{0:T(1024)}, s32[2048]{0:T(1024)S(1)}, u32[]{:S(2)}) copy-start(s32[2048]{0:T(1024)S(1)} %add_select_fusion.3) | copy-start | bytes 24580
  105.4 53.0 %copy-start.26 = (s32[256]{0:T(256)}, s32[256]{0:T(256)S(1)}, u32[]{:S(2)}) copy-start(s32[256]{0:T(256)S(1)} %add_bitcast_fusion) | copy-start | bytes 3076
  145.4 6.3 copy-start.28
  164.6 7.1 copy-start.1
  187.3 55.8 %all-to-all-start.6 = ((f32[2,2,128,2048]{3,0,1,2:T(2,128)}), f32[2,2,128,2048]{3,0,1,2:T(2,128)}, u32[]{:S(2)}, u32[]{:S(2)}) async-start(f32[2,2,128,2048]{3,0,1,2:T(2,128)} %copy.194), calls=%async_computation.6 | async-start | bytes 8388608 | tf_op jit(solution)/shard_map/all_to_all | solution.py:184
  506.5 8.3 copy-start.2
  506.5 8.3 copy-start.4
  514.8 5.4 copy-start.13
  678.7 4.8 copy-start.25
  678.7 31.1 %all-to-all-start.3 = ((f32[8,16,4096]{2,1,0:T(8,128)}), f32[8,16,4096]{2,1,0:T(8,128)}, u32[]{:S(2)}, u32[]{:S(2)}) async-start(f32[8,16,4096]{2,1,0:T(8,128)} %copy.179), calls=%async_computation.3 | async-start | bytes 4194304 | tf_op jit(solution)/shard_map/all_to_all | solution.py:189
  683.2 100.1 %reduce-scatter.2.cloned.1.call-start = ((), (), s32[]{:S(2)}) async-start(), calls=%async_computation.9 | async-start | bytes 1179648 | tf_op jit(solution)/shard_map/reduce_scatter | solution.py:218
  683.5 26.4 %copy-start.9 = (bf16[1,128,4096]{2,1,0:T(8,128)(2,1)S(1)}, bf16[1,128,4096]{2,1,0:T(8,128)(2,1)}, u32[]{:S(2)}) copy-start(bf16[1,128,4096]{2,1,0:T(8,128)(2,1)} %param.9) | copy-start | bytes 3145732
  709.8 3.8 copy-start.6
  713.6 4.2 copy-start.7
  713.6 7.3 slice-start
  714.3 3.4 collective-permute-start.1
  717.8 3.1 slice-start.1
  717.8 3.1 copy-start.16
  717.8 3.1 copy-start.18
  717.8 3.1 copy-start.20
  720.9 11.1 %copy-start.27 = (s32[256]{0:T(256)S(1)}, s32[256]{0:T(256)}, u32[]{:S(2)}) copy-start(s32[256]{0:T(256)} %copy-done.26) | copy-start | bytes 3076
  730.3 7.4 copy-start.22
  730.3 111.5 %collective-permute-start.2 = (bf16[3,128,4096]{2,1,0:T(8,128)(2,1)}, bf16[3,128,4096]{2,1,0:T(8,128)(2,1)S(1)}, u32[]{:S(2)}, u32[]{:S(2)}) collective-permute-start(bf16[3,128,4096]{2,1,0:T(8,128)(2,1)} %get-tuple-element.19), channel_id=1, source_target_pairs={{1,0},{2,1},{3,2},{5,4},{6,5},{7,6},{9,8},{10,9},{11,10},{13,12},{... | collective-permute-start | bytes 9437192 | tf_op jit(solution)/shard_map/ppermute | solution.py:13
  743.9 96.1 %all-reduce.2.cloned.1.call-start = ((), (), s32[]{:S(2)}) async-start(), calls=%async_computation.10 | async-start | bytes 393216 | tf_op jit(solution)/shard_map/psum | solution.py:215
  (9 other events, 18.0 us)
Sparse Core Ops, SparseCore 0:
  105.8 39.5 all-gather.2
  744.0 39.1 reduce-scatter.1
  786.3 53.6 all-reduce.1
where the time goes:
time: 862 us; the launch traced here: 850 us
  local copies, waits for them, and re-layouts  248 us (29%)
  waiting for transfers between devices  220 us (26%)
  blocking collectives  153 us (18%)
  other arithmetic  116 us (13%)
  matrix products  70.2 us (8%)
  starting transfers between devices  29 us (3%)
  between operations  15.1 us (2%)
    another operation x2, local copies, waits for them, and re-layouts, unpack_pairs(): joined = jnp.stack([pair_view[0], pair_view[1]], axis=-2)  60.9 us
    psum x1, waiting for transfers between devices, local(): tap_grads = lax.psum(tap_terms, 'seq') / math.sqrt(total_rows)  55.2 us
    all_to_all x1, blocking collectives, inverse(): lax.all_to_all(turned, 'seq', split_axis=2, concat_axis=1, tiled=True)  52.8 us
    all_to_all x1, blocking collectives, forward(): lax.all_to_all(turned, 'seq', split_axis=1, concat_axis=2, tiled=True)  51.9 us
    all_to_all x1, waiting for transfers between devices, inverse(): lax.all_to_all(turned, 'seq', split_axis=2, concat_axis=1, tiled=True)  49.7 us
    another operation x2, other arithmetic, unpack_pairs(): joined = jnp.stack([pair_view[0], pair_view[1]], axis=-2)  46 us
    all_gather x1, waiting for transfers between devices, local(): whole_filter = lax.all_gather(long_filter[0], 'seq', axis=0, tiled=True)  39.8 us
    reduce_scatter x1, waiting for transfers between devices, local(): lax.psum_scatter((matmul(cosine_part, cross_real) - matmul(sine_part, cro...  38.3 us
  transfers between devices with their start and end apart: 10, of which 8 were waited for; matrix products, arithmetic and copies ran while one was open for 5% of the time, Pallas kernels for 0%

commit v1 on v0

--- a/solution.py
+++ b/solution.py
@@ -5,6 +5,28 @@
 from jax.sharding import PartitionSpec as P
 
 exact_mode = lax.Precision.HIGHEST
+
+
+def in_blocks(shard, dim, length):
+    before, after = (shard.shape[:dim], shard.shape[dim + 1 :])
+    return jnp.moveaxis(shard.reshape(*before, length, -1, *after), dim, 0)
+
+
+def laid_out(pieces, dim):
+    lengths = list(pieces.shape[1:])
+    lengths[dim] *= pieces.shape[0]
+    return jnp.moveaxis(pieces, 0, dim).reshape(lengths)
+
+
+def exchange_in_pairs(x, axis, split_dim, concat_dim):
+    size, here = (lax.axis_size(axis), lax.axis_index(axis))
+    blocks = in_blocks(x, split_dim, size)
+    gathered = [blocks[here]]
+    for turn in range(1, size):
+        sent = blocks[here ^ turn]
+        gathered.append(lax.ppermute(sent, axis, [(i, i ^ turn) for i in range(size)]))
+    blocks = jnp.stack(gathered)[here ^ jnp.arange(size)]
+    return laid_out(blocks, concat_dim)
 
 
 def passed_along(x, axis, by):
@@ -171,7 +193,7 @@
             fft_length,
             1,
         )
-        gathered = lax.all_to_all(turned, "seq", split_axis=1, concat_axis=2, tiled=True)
+        gathered = exchange_in_pairs(turned, "seq", 1, 2)
         return middle_segment(gathered, counting(rows_dev), counting(rows_dev), rows_dev, 1)
 
     def inverse(spectrum):

time: 862 us -> 887 us (1.029)
  blocking collectives: 153 us -> 101 us
  waiting for transfers between devices: 220 us -> 256 us
  local copies, waits for them, and re-layouts: 248 us -> 278 us
  other arithmetic: 116 us -> 128 us
    ppermute x0 -> x14, waiting for transfers between devices: none -> 81.2 us  [exchange_in_pairs(): lax.ppermute(sent, axis, [(i, i ^ turn) for i in range(size)])]
    all_to_all x1 -> x0, blocking collectives: 51.9 us -> none  [forward(): lax.all_to_all(turned, 'seq', split_axis=1, concat_axis=2, tiled=True)]
    all_gather x1, waiting for transfers between devices: 39.8 us -> 0.01 us  [local(): whole_filter = lax.all_gather(long_filter[0], 'seq', axis=0, tiled=True)]
    unnamed x81 -> x113, local copies, waits for them, and re-layouts: 28.1 us -> 43.9 us
    ppermute x0 -> x14, starting transfers between devices: none -> 11.1 us  [exchange_in_pairs(): lax.ppermute(sent, axis, [(i, i ^ turn) for i in range(size)])]
    gather x0 -> x2, local copies, waits for them, and re-layouts: none -> 10 us  [exchange_in_pairs(): blocks = jnp.stack(gathered)[here ^ jnp.arange(size)]]
    unnamed x5 -> x7, other arithmetic: 17.1 us -> 18.7 us
  transfers between devices with their start and end apart: 10 -> 23, of which waited for: 8 -> 11; matrix products, arithmetic and copies ran while one was open for 5% -> 15% of each run, Pallas kernels for 0% -> 0%
where the time goes in v1:
time: 887 us; the launch traced here: 880 us
  local copies, waits for them, and re-layouts  278 us (31%)
  waiting for transfers between devices  256 us (29%)
  other arithmetic  128 us (14%)
  blocking collectives  101 us (11%)
  matrix products  70.5 us (8%)
  starting transfers between devices  31.2 us (4%)
  between operations  15 us (2%)
    ppermute x14, waiting for transfers between devices, exchange_in_pairs(): lax.ppermute(sent, axis, [(i, i ^ turn) for i in range(size)])  81.2 us
    another operation x2, local copies, waits for them, and re-layouts, unpack_pairs(): joined = jnp.stack([pair_view[0], pair_view[1]], axis=-2)  61 us
    psum x1, waiting for transfers between devices, local(): tap_grads = lax.psum(tap_terms, 'seq') / math.sqrt(total_rows)  55.2 us
    all_to_all x1, blocking collectives, inverse(): lax.all_to_all(turned, 'seq', split_axis=2, concat_axis=1, tiled=True)  53.1 us
    all_to_all x1, waiting for transfers between devices, inverse(): lax.all_to_all(turned, 'seq', split_axis=2, concat_axis=1, tiled=True)  49 us
    another operation x2, other arithmetic, unpack_pairs(): joined = jnp.stack([pair_view[0], pair_view[1]], axis=-2)  45.1 us
    unnamed x113, local copies, waits for them, and re-layouts  43.9 us
    reduce_scatter x1, waiting for transfers between devices, local(): lax.psum_scatter((matmul(cosine_part, cross_real) - matmul(sine_part, cro...  38.3 us
  transfers between devices with their start and end apart: 23, of which 11 were waited for; matrix products, arithmetic and copies ran while one was open for 15% of the time, Pallas kernels for 0%

profile of v1, /device:TPU:0, one launch (start us, length us, event | category | flops | bytes accessed | tf_op | source)
XLA Modules:
  0.0 880.3 jit_solution(14971334951093697117)
XLA Ops:
  49.8 10.3 %all-to-all-done.3 = bf16[8,2,32768]{2,1,0:T(2,128)(2,1)S(1)} async-done(((bf16[8,2,32768]{2,1,0:T(2,128)(2,1)}), bf16[8,2,32768]{2,1,0:T(2,128)(2,1)S(1)}, u32[]{:S(2)}, u32[]{:S(2)}) %all-to-all-start.3) | async-done | bytes 1048608 | tf_op jit(solution)/shard_map/all_to_all | solution.py:184
  66.1 8.5 reshape.451
  74.7 11.1 %fusion.168 = (f32[8,16,512,1,4]{1,0,4,3,2:T(8,128)}, f32[8,16,512,1,4]{1,0,4,3,2:T(8,128)}) fusion(f32[8,16,512,2,4]{1,0,4,3,2:T(8,128)} %reshape.451), kind=kLoop, calls=%fused_computation.301 | loop fusion | bytes 4194304 | tf_op jit(solution)/shard_map/slice | solution.py:92
  117.8 18.0 %collective-permute-done.9 = f32[2,2,16,2048]{3,2,1,0:T(8,128)S(1)} collective-permute-done((f32[2,2,16,2048]{3,2,1,0:T(8,128)S(1)}, f32[2,2,16,2048]{3,2,1,0:T(8,128)S(1)}, u32[]{:S(2)}, u32[]{:S(2)}) %collective-permute-start.9) | collective-permute-done | bytes 524320 | tf_op jit(solution)/shard_map/ppermute | solution.py:27
  136.7 20.7 %collective-permute-done.10 = f32[2,2,16,2048]{3,2,1,0:T(8,128)S(1)} collective-permute-done((f32[2,2,16,2048]{3,2,1,0:T(8,128)S(1)}, f32[2,2,16,2048]{3,2,1,0:T(8,128)S(1)}, u32[]{:S(2)}, u32[]{:S(2)}) %collective-permute-start.10) | collective-permute-done | bytes 524320 | tf_op jit(solution)/shard_map/ppermute | solution.py:27
  169.1 8.7 fusion.18
  201.3 7.3 copy.164
  213.5 49.0 %all-to-all-done.4 = f32[2,2,128,2048]{3,0,1,2:T(2,128)} async-done(((f32[2,2,128,2048]{3,0,1,2:T(2,128)}), f32[2,2,128,2048]{3,0,1,2:T(2,128)}, u32[]{:S(2)}, u32[]{:S(2)}) %all-to-all-start.4) | async-done | bytes 4194336 | tf_op jit(solution)/shard_map/all_to_all | solution.py:206
  272.3 8.9 %copy.167 = f32[8,32768]{0,1:T(8,128)} copy(f32[8,32768]{1,0:T(8,128)S(1)} %get-tuple-element.49) | data formatting | bytes 2097152 | tf_op jit(solution)/shard_map/slice | solution.py:101
  281.2 8.9 %copy.168 = f32[8,32768]{0,1:T(8,128)} copy(f32[8,32768]{1,0:T(8,128)S(1)} %get-tuple-element.50) | data formatting | bytes 2097152 | tf_op jit(solution)/shard_map/slice | solution.py:101
  290.1 22.6 %pad_maximum_fusion.1 = f32[8,16,512,2,4]{0,4,2,1,3:T(4,128)} fusion(f32[8,16,512,1,4]{0,4,2,1,3:T(4,128)} %bitcast.227, f32[8,16,512,1,4]{0,4,2,1,3:T(4,128)} %bitcast.225), kind=kLoop, calls=%fused_computation.3 | loop fusion | flops 524288 | bytes 4194304 | tf_op jit(solution)/shard_map/stack | solution.py:101
  312.7 30.5 %copy.169 = f32[8,16,512,2,4]{1,0,4,3,2:T(8,128)} copy(f32[8,16,512,2,4]{0,4,2,1,3:T(4,128)} %pad_maximum_fusion.1) | data formatting | bytes 4194304 | tf_op jit(solution)/shard_map/stack | solution.py:101
  343.1 9.6 %copy.170 = f32[8,16,4096]{2,1,0:T(8,128)S(1)} copy(f32[8,16,4096]{1,0,2:T(8,128)} %bitcast.223) | data formatting | bytes 4194304 | tf_op jit(solution)/shard_map/reshape | solution.py:102
  352.8 29.4 %all_to_all.66 = f32[8,16,4096]{2,1,0:T(8,128)S(1)} all-to-all(f32[8,16,4096]{2,1,0:T(8,128)S(1)} %copy.170), channel_id=1, replica_groups=mesh['seq'=8,'pipe'=4] {'seq'}, dimensions={0} | all-to-all | bytes 4194304 | tf_op jit(solution)/shard_map/all_to_all | solution.py:211
  389.9 8.4 reduce.1
  399.8 18.8 %all_to_all.67 = bf16[8,2,32768]{2,1,0:T(2,128)(2,1)S(1)} all-to-all(bf16[8,2,32768]{2,1,0:T(2,128)(2,1)} %reshape.482), channel_id=1, replica_groups=mesh['seq'=8,'pipe'=4] {'seq'}, dimensions={0} | all-to-all | bytes 2097152 | tf_op jit(solution)/shard_map/all_to_all | solution.py:184
  429.5 10.6 %reshape.450 = f32[8,16,512,2,4]{1,0,4,3,2:T(8,128)} reshape(f32[1,128,4096]{1,2,0:T(8,128)} %copy.139) | data formatting | bytes 4194304 | tf_op jit(solution)/shard_map/convert_element_type | solution.py:185
  440.0 11.1 %fusion.169 = (f32[8,16,512,1,4]{1,0,4,3,2:T(8,128)}, f32[8,16,512,1,4]{1,0,4,3,2:T(8,128)}) fusion(f32[8,16,512,2,4]{1,0,4,3,2:T(8,128)} %reshape.450), kind=kLoop, calls=%fused_computation.302 | loop fusion | bytes 4194304 | tf_op jit(solution)/shard_map/slice | solution.py:92
  479.5 7.8 collective-permute-done.2
  488.2 31.8 %collective-permute-done.3 = f32[2,2,16,2048]{3,2,1,0:T(8,128)S(1)} collective-permute-done((f32[2,2,16,2048]{3,2,1,0:T(8,128)S(1)}, f32[2,2,16,2048]{3,2,1,0:T(8,128)S(1)}, u32[]{:S(2)}, u32[]{:S(2)}) %collective-permute-start.3) | collective-permute-done | bytes 524320 | tf_op jit(solution)/shard_map/ppermute | solution.py:27
  534.5 8.5 fusion.15
  556.2 7.3 copy.148
  563.6 53.1 %all_to_all.68 = f32[2,2,128,2048]{3,0,1,2:T(2,128)S(1)} all-to-all(f32[2,2,128,2048]{3,0,1,2:T(2,128)} %copy.148), channel_id=1, replica_groups=mesh['seq'=8,'pipe'=4] {'seq'}, dimensions={2} | all-to-all | bytes 8388608 | tf_op jit(solution)/shard_map/all_to_all | solution.py:206
  625.2 9.2 %copy.151 = f32[8,32768]{0,1:T(8,128)} copy(f32[8,32768]{1,0:T(8,128)} %get-tuple-element.51) | data formatting | bytes 2097152 | tf_op jit(solution)/shard_map/slice | solution.py:101
  634.4 8.9 %copy.152 = f32[8,32768]{0,1:T(8,128)} copy(f32[8,32768]{1,0:T(8,128)S(1)} %get-tuple-element.52) | data formatting | bytes 2097152 | tf_op jit(solution)/shard_map/slice | solution.py:101
  643.2 22.6 %pad_maximum_fusion = f32[8,16,512,2,4]{0,4,2,1,3:T(4,128)} fusion(f32[8,16,512,1,4]{0,4,2,1,3:T(4,128)} %bitcast.228, f32[8,16,512,1,4]{0,4,2,1,3:T(4,128)} %bitcast.226), kind=kLoop, calls=%fused_computation.2 | loop fusion | flops 524288 | bytes 4194304 | tf_op jit(solution)/shard_map/stack | solution.py:101
  665.8 30.5 %copy.153 = f32[8,16,512,2,4]{1,0,4,3,2:T(8,128)} copy(f32[8,16,512,2,4]{0,4,2,1,3:T(4,128)} %pad_maximum_fusion) | data formatting | bytes 4194304 | tf_op jit(solution)/shard_map/stack | solution.py:101
  696.3 10.6 %copy.154 = f32[8,16,4096]{2,1,0:T(8,128)} copy(f32[8,16,4096]{1,0,2:T(8,128)} %bitcast.224) | data formatting | bytes 4194304 | tf_op jit(solution)/shard_map/reshape | solution.py:102
  718.2 19.8 %all-to-all-done.2 = f32[8,16,4096]{2,1,0:T(8,128)} async-done(((f32[8,16,4096]{2,1,0:T(8,128)}), f32[8,16,4096]{2,1,0:T(8,128)}, u32[]{:S(2)}, u32[]{:S(2)}) %all-to-all-start.2) | async-done | bytes 2097184 | tf_op jit(solution)/shard_map/all_to_all | solution.py:211
  751.0 9.4 %multiply_reduce_fusion.2 = (f32[3,4096]{1,0:T(4,128)S(1)}, f32[3,4096]{1,0:T(4,128)S(1)}, f32[3,4096]{1,0:T(4,128)S(1)}, bf16[3,128,4096]{2,1,0:T(8,128)(2,1)}) fusion(f32[3,130,4096]{2,1,0:T(8,128)S(1)} %bitcast.222, f32[1,128,4096]{2,1,0:T(8,128)} %get-tuple-element.14, f32[1,128,4096]{2,1,0:T(8,128)S(1)} %get-tuple-element.13, ...), kind=kLoop, calls=%fused_computation.45 | loop fusion | flops 21983232 | bytes 41189376 | tf_op jit(solution)/shard_map/reduce_sum | solution.py:232
  775.1 38.3 %reduce-scatter.2.cloned.1.call-done = f32[128,256]{1,0:T(8,128)} async-done(((f32[1024,256]{1,0:T(8,128)}), f32[128,256]{1,0:T(8,128)}) %reduce-scatter.2.cloned.1.call-update) | async-done | bytes 131088 | tf_op jit(solution)/shard_map/reduce_scatter | solution.py:240
  814.9 55.2 %all-reduce.2.cloned.1.call-done = f32[3,3,4096]{2,1,0:T(4,128)} async-done(((f32[3,3,4096]{2,1,0:T(4,128)}), f32[3,3,4096]{2,1,0:T(4,128)}) %all-reduce.2.cloned.1.call-update) | async-done | bytes 147472 | tf_op jit(solution)/shard_map/psum | solution.py:237
  (249 shorter events, 260.1 us)
Async XLA Ops:
  7.2 13.3 %copy-start.31 = (f32[1,3,3,4096]{3,0,2,1:T(1,128)S(1)}, f32[1,3,3,4096]{3,0,2,1:T(1,128)}, u32[]{:S(2)}) copy-start(f32[1,3,3,4096]{3,0,2,1:T(1,128)} %param.11) | copy-start | bytes 442372
  7.2 170.6 %all-gather.3.cloned.1.call-start = ((), (), s32[]{:S(2)}) async-start(), calls=%async_computation.9 | async-start | bytes 1179648 | tf_op jit(solution)/shard_map/all_gather | solution.py:176
  11.4 10.0 %collective-permute-start = (bf16[3,2,4096]{2,1,0:T(2,128)(2,1)}, bf16[3,2,4096]{2,1,0:T(2,128)(2,1)}, u32[]{:S(2)}, u32[]{:S(2)}) collective-permute-start(bf16[3,2,4096]{2,1,0:T(2,128)(2,1)} %slice.194), channel_id=1, source_target_pairs={{0,4},{4,8},{8,12},{12,16},{16,20},{20,24},{24,28},{1,5},{5,9},{9,... | collective-permute-start | bytes 147464 | tf_op jit(solution)/shard_map/ppermute | solution.py:35
  40.2 20.0 %all-to-all-start.3 = ((bf16[8,2,32768]{2,1,0:T(2,128)(2,1)}), bf16[8,2,32768]{2,1,0:T(2,128)(2,1)S(1)}, u32[]{:S(2)}, u32[]{:S(2)}) async-start(bf16[8,2,32768]{2,1,0:T(2,128)(2,1)} %reshape.484), calls=%async_computation.3 | async-start | bytes 2097152 | tf_op jit(solution)/shard_map/all_to_all | solution.py:184
  48.2 135.8 %copy-start.35 = (s32[256]{0:T(256)}, s32[256]{0:T(256)S(1)}, u32[]{:S(2)}) copy-start(s32[256]{0:T(256)S(1)} %add_bitcast_fusion) | copy-start | bytes 3076
  107.6 7.2 collective-permute-start.8
  107.8 61.3 %copy-start.14 = (f32[2,128,2,128]{3,2,1,0:T(2,128)}, f32[2,128,2,128]{3,2,1,0:T(2,128)S(1)}, u32[]{:S(2)}) copy-start(f32[2,128,2,128]{3,2,1,0:T(2,128)S(1)} %reshape.442) | copy-start | bytes 786436
  108.0 87.1 %copy-start.12 = (f32[2,128,2,128]{3,2,1,0:T(2,128)}, f32[2,128,2,128]{3,2,1,0:T(2,128)S(1)}, u32[]{:S(2)}) copy-start(f32[2,128,2,128]{3,2,1,0:T(2,128)S(1)} %reshape.443) | copy-start | bytes 786436
  108.0 27.8 %copy-start.25 = (f32[2,2,16,2048]{3,2,1,0:T(8,128)S(1)}, f32[2,2,16,2048]{3,2,1,0:T(8,128)}, u32[]{:S(2)}) copy-start(f32[2,2,16,2048]{3,2,1,0:T(8,128)} %get-tuple-element.36) | copy-start | bytes 1572868
  109.2 50.7 %collective-permute-start.13 = (f32[2,2,16,2048]{3,2,1,0:T(8,128)S(1)}, f32[2,2,16,2048]{3,2,1,0:T(8,128)S(1)}, u32[]{:S(2)}, u32[]{:S(2)}) collective-permute-start(f32[2,2,16,2048]{3,2,1,0:T(8,128)S(1)} %fusion.70), channel_id=1, source_target_pairs={{0,24},{4,28},{8,16},{12,20},{16,8},{20,12},{24,0},{28,4},{1,25},{... | collective-permute-start | bytes 1572872 | tf_op jit(solution)/shard_map/ppermute | solution.py:27
  110.4 25.4 %collective-permute-start.9 = (f32[2,2,16,2048]{3,2,1,0:T(8,128)S(1)}, f32[2,2,16,2048]{3,2,1,0:T(8,128)S(1)}, u32[]{:S(2)}, u32[]{:S(2)}) collective-permute-start(f32[2,2,16,2048]{3,2,1,0:T(8,128)S(1)} %copy-done.28), channel_id=1, source_target_pairs={{0,8},{4,12},{8,0},{12,4},{16,24},{20,28},{24,16},{28,20},{1,9},{5... | collective-permute-start | bytes 1572872 | tf_op jit(solution)/shard_map/ppermute | solution.py:27
  112.6 48.1 %collective-permute-start.14 = (f32[2,2,16,2048]{3,2,1,0:T(8,128)S(1)}, f32[2,2,16,2048]{3,2,1,0:T(8,128)S(1)}, u32[]{:S(2)}, u32[]{:S(2)}) collective-permute-start(f32[2,2,16,2048]{3,2,1,0:T(8,128)S(1)} %copy-done.24), channel_id=1, source_target_pairs={{0,28},{4,24},{8,20},{12,16},{16,12},{20,8},{24,4},{28,0},{1,29},{... | collective-permute-start | bytes 1572872 | tf_op jit(solution)/shard_map/ppermute | solution.py:27
  113.2 44.2 %collective-permute-start.10 = (f32[2,2,16,2048]{3,2,1,0:T(8,128)S(1)}, f32[2,2,16,2048]{3,2,1,0:T(8,128)S(1)}, u32[]{:S(2)}, u32[]{:S(2)}) collective-permute-start(f32[2,2,16,2048]{3,2,1,0:T(8,128)S(1)} %copy-done.27), channel_id=1, source_target_pairs={{0,12},{4,8},{8,4},{12,0},{16,28},{20,24},{24,20},{28,16},{1,13},{... | collective-permute-start | bytes 1572872 | tf_op jit(solution)/shard_map/ppermute | solution.py:27
  114.9 43.4 %collective-permute-start.11 = (f32[2,2,16,2048]{3,2,1,0:T(8,128)S(1)}, f32[2,2,16,2048]{3,2,1,0:T(8,128)S(1)}, u32[]{:S(2)}, u32[]{:S(2)}) collective-permute-start(f32[2,2,16,2048]{3,2,1,0:T(8,128)S(1)} %copy-done.26), channel_id=1, source_target_pairs={{0,16},{4,20},{8,24},{12,28},{16,0},{20,4},{24,8},{28,12},{1,17},{... | collective-permute-start | bytes 1572872 | tf_op jit(solution)/shard_map/ppermute | solution.py:27
  135.8 23.3 %collective-permute-start.12 = (f32[2,2,16,2048]{3,2,1,0:T(8,128)S(1)}, f32[2,2,16,2048]{3,2,1,0:T(8,128)S(1)}, u32[]{:S(2)}, u32[]{:S(2)}) collective-permute-start(f32[2,2,16,2048]{3,2,1,0:T(8,128)S(1)} %copy-done.25), channel_id=1, source_target_pairs={{0,20},{4,16},{8,28},{12,24},{16,4},{20,0},{24,12},{28,8},{1,21},{... | collective-permute-start | bytes 1572872 | tf_op jit(solution)/shard_map/ppermute | solution.py:27
  177.8 13.2 %copy-start.33 = (s32[2048]{0:T(1024)S(1)}, s32[2048]{0:T(1024)}, u32[]{:S(2)}) copy-start(s32[2048]{0:T(1024)} %add_select_fusion.3) | copy-start | bytes 24580
  184.1 8.9 %copy-start.1 = (f32[2,2,128,2048]{2,3,0,1:T(8,128)S(1)}, f32[2,2,128,2048]{2,3,0,1:T(8,128)}, u32[]{:S(2)}) copy-start(f32[2,2,128,2048]{2,3,0,1:T(8,128)} %fusion.18) | copy-start | bytes 12582916
  208.6 53.9 %all-to-all-start.4 = ((f32[2,2,128,2048]{3,0,1,2:T(2,128)}), f32[2,2,128,2048]{3,0,1,2:T(2,128)}, u32[]{:S(2)}, u32[]{:S(2)}) async-start(f32[2,2,128,2048]{3,0,1,2:T(2,128)} %copy.164), calls=%async_computation.4 | async-start | bytes 8388608 | tf_op jit(solution)/shard_map/all_to_all | solution.py:206
  472.4 5.7 collective-permute-start.1
  472.5 14.9 %collective-permute-start.2 = (f32[2,2,16,2048]{3,2,1,0:T(8,128)S(1)}, f32[2,2,16,2048]{3,2,1,0:T(8,128)S(1)}, u32[]{:S(2)}, u32[]{:S(2)}) collective-permute-start(f32[2,2,16,2048]{3,2,1,0:T(8,128)S(1)} %get-tuple-element.41), channel_id=1, source_target_pairs={{0,8},{4,12},{8,0},{12,4},{16,24},{20,28},{24,16},{28,20},{1,9},{5... | collective-permute-start | bytes 1572872 | tf_op jit(solution)/shard_map/ppermute | solution.py:27
  474.0 51.3 %collective-permute-start.6 = (f32[2,2,16,2048]{3,2,1,0:T(8,128)S(1)}, f32[2,2,16,2048]{3,2,1,0:T(8,128)S(1)}, u32[]{:S(2)}, u32[]{:S(2)}) collective-permute-start(f32[2,2,16,2048]{3,2,1,0:T(8,128)S(1)} %fusion.87), channel_id=1, source_target_pairs={{0,24},{4,28},{8,16},{12,20},{16,8},{20,12},{24,0},{28,4},{1,25},{... | collective-permute-start | bytes 1572872 | tf_op jit(solution)/shard_map/ppermute | solution.py:27
  475.5 50.7 %collective-permute-start.7 = (f32[2,2,16,2048]{3,2,1,0:T(8,128)S(1)}, f32[2,2,16,2048]{3,2,1,0:T(8,128)S(1)}, u32[]{:S(2)}, u32[]{:S(2)}) collective-permute-start(f32[2,2,16,2048]{3,2,1,0:T(8,128)S(1)} %get-tuple-element.39), channel_id=1, source_target_pairs={{0,28},{4,24},{8,20},{12,16},{16,12},{20,8},{24,4},{28,0},{1,29},{... | collective-permute-start | bytes 1572872 | tf_op jit(solution)/shard_map/ppermute | solution.py:27
  476.4 43.6 %collective-permute-start.3 = (f32[2,2,16,2048]{3,2,1,0:T(8,128)S(1)}, f32[2,2,16,2048]{3,2,1,0:T(8,128)S(1)}, u32[]{:S(2)}, u32[]{:S(2)}) collective-permute-start(f32[2,2,16,2048]{3,2,1,0:T(8,128)S(1)} %get-tuple-element.42), channel_id=1, source_target_pairs={{0,12},{4,8},{8,4},{12,0},{16,28},{20,24},{24,20},{28,16},{1,13},{... | collective-permute-start | bytes 1572872 | tf_op jit(solution)/shard_map/ppermute | solution.py:27
  478.1 42.7 %collective-permute-start.4 = (f32[2,2,16,2048]{3,2,1,0:T(8,128)S(1)}, f32[2,2,16,2048]{3,2,1,0:T(8,128)S(1)}, u32[]{:S(2)}, u32[]{:S(2)}) collective-permute-start(f32[2,2,16,2048]{3,2,1,0:T(8,128)S(1)} %get-tuple-element.43), channel_id=1, source_target_pairs={{0,16},{4,20},{8,24},{12,28},{16,0},{20,4},{24,8},{28,12},{1,17},{... | collective-permute-start | bytes 1572872 | tf_op jit(solution)/shard_map/ppermute | solution.py:27
  487.3 37.1 %collective-permute-start.5 = (f32[2,2,16,2048]{3,2,1,0:T(8,128)S(1)}, f32[2,2,16,2048]{3,2,1,0:T(8,128)S(1)}, u32[]{:S(2)}, u32[]{:S(2)}) collective-permute-start(f32[2,2,16,2048]{3,2,1,0:T(8,128)S(1)} %get-tuple-element.44), channel_id=1, source_target_pairs={{0,20},{4,16},{8,28},{12,24},{16,4},{20,0},{24,12},{28,8},{1,21},{... | collective-permute-start | bytes 1572872 | tf_op jit(solution)/shard_map/ppermute | solution.py:27
  706.9 31.1 %all-to-all-start.2 = ((f32[8,16,4096]{2,1,0:T(8,128)}), f32[8,16,4096]{2,1,0:T(8,128)}, u32[]{:S(2)}, u32[]{:S(2)}) async-start(f32[8,16,4096]{2,1,0:T(8,128)} %copy.154), calls=%async_computation.2 | async-start | bytes 4194304 | tf_op jit(solution)/shard_map/all_to_all | solution.py:211
  711.4 26.6 %copy-start.11 = (bf16[1,128,4096]{2,1,0:T(8,128)(2,1)S(1)}, bf16[1,128,4096]{2,1,0:T(8,128)(2,1)}, u32[]{:S(2)}) copy-start(bf16[1,128,4096]{2,1,0:T(8,128)(2,1)} %param.9) | copy-start | bytes 3145732
  711.4 102.0 %reduce-scatter.2.cloned.1.call-start = ((), (), s32[]{:S(2)}) async-start(), calls=%async_computation.7 | async-start | bytes 1179648 | tf_op jit(solution)/shard_map/reduce_scatter | solution.py:240
  742.5 3.1 collective-permute-start.15
  751.0 11.0 %copy-start.36 = (s32[256]{0:T(256)S(1)}, s32[256]{0:T(256)}, u32[]{:S(2)}) copy-start(s32[256]{0:T(256)} %copy-done.35) | copy-start | bytes 3076
  760.4 111.5 %collective-permute-start.16 = (bf16[3,128,4096]{2,1,0:T(8,128)(2,1)}, bf16[3,128,4096]{2,1,0:T(8,128)(2,1)S(1)}, u32[]{:S(2)}, u32[]{:S(2)}) collective-permute-start(bf16[3,128,4096]{2,1,0:T(8,128)(2,1)} %get-tuple-element.19), channel_id=1, source_target_pairs={{1,0},{2,1},{3,2},{5,4},{6,5},{7,6},{9,8},{10,9},{11,10},{13,12},{... | collective-permute-start | bytes 9437192 | tf_op jit(solution)/shard_map/ppermute | solution.py:35
  774.1 96.1 %all-reduce.2.cloned.1.call-start = ((), (), s32[]{:S(2)}) async-start(), calls=%async_computation.8 | async-start | bytes 393216 | tf_op jit(solution)/shard_map/psum | solution.py:237
  (32 other events, 130.3 us)
Sparse Core Ops, SparseCore 0:
  9.9 26.1 all-gather.2
  774.2 39.1 reduce-scatter.1
  816.4 53.6 all-reduce.1
